TPU v7x, 32 devices: a whole 2x2x4 slice. The times are simulated.
32 devices in a mesh: space: 32 (over z, y, x, core), dp: 1.
Axes of the slice: x: 2, y: 2, z: 4, core: 2. Of those that a mesh axis runs over, the one named last changes fastest.
Arguments:
- activations: bfloat16 [1, 128, 16, 16, 128], P('dp', 'space'), may hold values from -100 to 100
- upstream: bfloat16 [1, 128, 16, 16, 128], P('dp', 'space'), may hold values from -100 to 100
- kernel_weight: bfloat16 [27, 128, 128], replicated, may hold values from -0.109375 to 0.109375
- patch_inverse: float32 [27, 128, 3456], P(None, 'space'), may hold values from -0.1 to 1.6, as said below
- output_inverse: float32 [128, 128], replicated, may hold values from -0.1 to 1.6, as said below
Outputs:
- activated: bfloat16 [1, 128, 16, 16, 128], P('dp', 'space')
- input_grad: bfloat16 [1, 128, 16, 16, 128], P('dp', 'space')
- patch_factor: float32 [128, 63, 128], P('space', None, 'dp')
- output_factor: float32 [128, 128], replicated
- precond_grad: float32 [27, 128, 128], P(None, 'space')
Inputs may be any that keep to these rules, and one draw needn't show every extreme that they name: Symmetric as a 3456 x 3456 matrix whose row o * 128 + c is patch_inverse[o, c, :]. `output_inverse`: symmetric.
All inputs are finite; a program needn't handle non-finite values.
Results may differ from a plain program's by a relative error of at most 0.0015.
The roundings to bfloat16 on the way count: a program that leaves them out, or rounds other values in their place, can miss the bound.
Values may be sent and summed in bfloat16 or wider, within the bound.
No kernel may reach another device: no remote copies, remote signals or barrier semaphores. Data moves between devices by JAX's collectives and lax.ppermute only.
A program may use at most 128 MiB of HBM per device.

v0:
```python
import jax
import jax.numpy as jnp
from jax import lax
from jax.sharding import PartitionSpec as P


def padded_2(shard, sides, width):
    for axis, dim in sides:
        peers, length = (lax.axis_size(axis), shard.shape[dim])
        up = [(i, (i + 1) % peers) for i in range(peers)]
        down = [(j, i) for i, j in up]
        last = lax.slice_in_dim(shard, length - width, length, axis=dim)
        leading = lax.slice_in_dim(shard, 0, width, axis=dim)
        before = lax.ppermute(last, axis, up)
        after = lax.ppermute(leading, axis, down)
        shard = jnp.concatenate([before, shard, after], axis=dim)
    return shard


def tap_shift(offset):
    return (offset // 9 - 1, offset // 3 % 3 - 1, offset % 3 - 1)


def lag_shift(lag):
    number = lag + 62
    return (number // 25 - 2, number // 5 % 5 - 2, number % 5 - 2)


def window(padded, depth, shift_z, shift_y, shift_x):
    piece = padded[:, 1 + shift_z : 1 + shift_z + depth]
    piece = jnp.roll(piece, (-shift_y, -shift_x), axis=(2, 3))
    return piece.reshape(-1, piece.shape[-1])


def inner_rows(left_rows, right_rows):
    return lax.dot_general(
        left_rows, right_rows, (((0,), (0,)), ((), ())), preferred_element_type=jnp.float32
    )


def per_device(activations, upstream, kernel_weight, patch_inverse, output_inverse):
    depth = activations.shape[1]
    chans = activations.shape[-1]
    cells = depth * activations.shape[2] * activations.shape[3]
    total = float(cells * lax.axis_size("space") * lax.axis_size("dp"))
    padded = padded_2(activations, (("space", 1),), 1)
    pre = jnp.zeros((cells, chans), jnp.float32)
    for offset in range(27):
        displacement = tap_shift(offset)
        moved = window(padded, depth, displacement[0], displacement[1], displacement[2])
        pre = pre + jnp.dot(moved, kernel_weight[offset], preferred_element_type=jnp.float32)
    logistic = jax.nn.sigmoid(pre)
    activated = (pre * logistic).astype(jnp.bfloat16).reshape(activations.shape)
    slope = (
        upstream.reshape(cells, chans).astype(jnp.float32)
        * logistic
        * (1.0 + pre * (1.0 - logistic))
    ).astype(jnp.bfloat16)
    slope_padded = padded_2(slope.reshape(activations.shape), (("space", 1),), 1)
    back = jnp.zeros((cells, chans), jnp.float32)
    grads = []
    for offset in range(27):
        displacement = tap_shift(offset)
        slope_moved = window(
            slope_padded, depth, -displacement[0], -displacement[1], -displacement[2]
        )
        back = back + lax.dot_general(
            slope_moved,
            kernel_weight[offset],
            (((1,), (1,)), ((), ())),
            preferred_element_type=jnp.float32,
        )
        moved = window(padded, depth, displacement[0], displacement[1], displacement[2])
        grads.append(inner_rows(moved, slope))
    input_grad = back.astype(jnp.bfloat16).reshape(activations.shape)
    weight_local = jnp.stack(grads, axis=0) / total
    factor_local = inner_rows(slope, slope) / total
    weight_grad, output_factor = lax.psum((weight_local, factor_local), ("space", "dp"))
    blocks = []
    for lag in range(63):
        displacement = lag_shift(lag)
        left_z = -1 if displacement[0] == 2 else 0
        left = window(padded, depth, left_z, 0, 0)
        right = window(padded, depth, displacement[0] + left_z, displacement[1], displacement[2])
        blocks.append(inner_rows(left, right))
    owned_rows = lax.psum_scatter(
        jnp.stack(blocks, axis=1) / total, "space", scatter_dimension=0, tiled=True
    )
    patch_factor = lax.psum_scatter(owned_rows, "dp", scatter_dimension=2, tiled=True)
    owned = patch_inverse.shape[1]
    inverse_rows = patch_inverse.reshape(-1, patch_inverse.shape[-1])
    left_product = jnp.dot(
        inverse_rows, weight_grad.reshape(-1, chans), precision=lax.Precision.HIGHEST
    )
    precond_grad = jnp.dot(left_product, output_inverse, precision=lax.Precision.HIGHEST).reshape(
        27, owned, chans
    )
    return (activated, input_grad, patch_factor, output_factor, precond_grad)


def solution(mesh):
    return jax.shard_map(
        per_device,
        mesh=mesh,
        in_specs=(
            P("dp", "space", None, None, None),
            P("dp", "space", None, None, None),
            P(),
            P(None, "space", None),
            P(),
        ),
        out_specs=(
            P("dp", "space", None, None, None),
            P("dp", "space", None, None, None),
            P("space", None, "dp"),
            P(),
            P(None, "space", None),
        ),
        check_vma=False,
    )
```

profile of v0, /device:TPU:0, one launch (start us, length us, event | category | flops | bytes accessed | tf_op | source)
XLA Modules:
  0.0 283.5 jit_solution(16292431694442266520)
XLA Ops:
  7.2 1.6 fusion.499
  9.3 5.9 %collective-permute-start.1 = (bf16[1,1,16,16,128]{4,3,2,1,0:T(8,128)(2,1)}, bf16[1,1,16,16,128]{4,3,2,1,0:T(8,128)(2,1)}, u32[]{:S(2)}, u32[]{:S(2)}) collective-permute-start(bf16[1,1,16,16,128]{4,3,2,1,0:T(8,128)(2,1)} %get-tuple-element.165), channel_id=1, source_target_pairs={{1,0},{2,1},{3,2},{4,3},{5,4},{6,5},{7,6},{8,7},{9,8},{10,9},{11,1... | collective-permute-start | bytes 196616 | tf_op jit(solution)/shard_map/ppermute | solution.py:15
  15.2 1.1 fusion.495
  23.0 0.9 fusion.90
  24.8 0.9 fusion.88
  25.8 0.9 fusion.87
  26.7 0.9 fusion.86
  27.7 0.9 fusion.85
  28.6 0.9 fusion.84
  29.5 0.9 fusion.83
  31.4 0.9 fusion.81
  32.3 2.0 reshape.644
  34.3 1.1 pad_maximum_fusion.21
  35.4 1.9 fusion.80
  37.3 1.8 fusion.79
  50.7 1.1 fusion.93
  59.4 1.4 broadcast_multiply_fusion.1
  60.9 0.9 fusion.78
  64.5 0.9 fusion.74
  68.1 0.9 fusion.70
  69.9 0.9 fusion.68
  75.4 0.9 fusion.62
  76.3 0.9 fusion.61
  79.9 0.9 fusion.57
  80.8 0.9 fusion.56
  106.0 4.7 %broadcast_multiply_fusion = f32[128,63,128]{2,0,1:T(8,128)} fusion(f32[128,63,128]{2,0,1:T(8,128)} %fusion.29), kind=kLoop, calls=%fused_computation | loop fusion | flops 1032192 | bytes 8257536 | tf_op jit(solution)/shard_map/div | solution.py:87
  113.3 5.6 %collective-permute-done.3 = bf16[1,1,16,16,128]{4,3,2,1,0:T(8,128)(2,1)S(1)} collective-permute-done((bf16[1,1,16,16,128]{4,3,2,1,0:T(8,128)(2,1)S(1)}, bf16[1,1,16,16,128]{4,3,2,1,0:T(8,128)(2,1)S(1)}, u32[]{:S(2)}, u32[]{:S(2)}) %collective-permute-start.3) | collective-permute-done | bytes 65568 | tf_op jit(solution)/shard_map/ppermute | solution.py:14
  129.1 0.9 fusion.1
  130.0 137.7 %all-reduce.4.cloned.1.call-done = (f32[128,63,128]{2,0,1:T(8,128)}, f32[128,128]{1,0:T(8,128)}, f32[3456,128]{1,0:T(8,128)}) async-done(((f32[128,63,128]{2,0,1:T(8,128)}, f32[128,128]{1,0:T(8,128)}, f32[3456,128]{1,0:T(8,128)}), (f32[128,63,128]{2,0,1:T(8,128)}, f32[128,128]{1,0:T(8,128)}, f32[3456,128]{1,0:T(8,128)})) %all-reduce.4.cloned.1.call-update) | async-done | bytes 5963792
  267.8 4.4 %fusion.500 = f32[128,108]{1,0:T(8,128)S(1)} fusion(f32[3456,128]{1,0:T(8,128)} %get-tuple-element.7, f32[108,3456]{1,0:T(8,128)S(1)} %reshape.644), kind=kOutput, calls=%fused_computation.865 | convolution fusion | flops 573308928 | bytes 3317760 | tf_op jit(solution)/shard_map/dot_general | solution.py:92
  273.1 1.6 constant_dynamic-slice_fusion
  274.7 1.5 copy.279
  (248 shorter events, 78.6 us)
Async XLA Ops:
  7.2 265.0 %copy-start = (f32[128,128]{1,0:T(8,128)S(1)}, f32[128,128]{1,0:T(8,128)}, u32[]{:S(2)}) copy-start(f32[128,128]{1,0:T(8,128)} %param.9) | copy-start | bytes 196612
  7.2 11.8 %copy-start.1 = (bf16[1,4,16,16,128]{4,3,2,1,0:T(8,128)(2,1)S(1)}, bf16[1,4,16,16,128]{4,3,2,1,0:T(8,128)(2,1)}, u32[]{:S(2)}) copy-start(bf16[1,4,16,16,128]{4,3,2,1,0:T(8,128)(2,1)} %param.5) | copy-start | bytes 786436
  7.2 260.6 %all-reduce.4.cloned.1.call-start = ((), (), s32[]{:S(2)}) async-start(), calls=%async_computation | async-start | bytes 11927552
  8.8 30.4 %collective-permute-start = (bf16[1,1,16,16,128]{4,3,2,1,0:T(8,128)(2,1)}, bf16[1,1,16,16,128]{4,3,2,1,0:T(8,128)(2,1)}, u32[]{:S(2)}, u32[]{:S(2)}) collective-permute-start(bf16[1,1,16,16,128]{4,3,2,1,0:T(8,128)(2,1)} %get-tuple-element.164), channel_id=1, source_target_pairs={{0,1},{1,2},{2,3},{3,4},{4,5},{5,6},{6,7},{7,8},{8,9},{9,10},{10,1... | collective-permute-start | bytes 196616 | tf_op jit(solution)/shard_map/ppermute | solution.py:14
  9.3 31.5 %collective-permute-start.1 = (bf16[1,1,16,16,128]{4,3,2,1,0:T(8,128)(2,1)}, bf16[1,1,16,16,128]{4,3,2,1,0:T(8,128)(2,1)}, u32[]{:S(2)}, u32[]{:S(2)}) collective-permute-start(bf16[1,1,16,16,128]{4,3,2,1,0:T(8,128)(2,1)} %get-tuple-element.165), channel_id=1, source_target_pairs={{1,0},{2,1},{3,2},{4,3},{5,4},{6,5},{7,6},{8,7},{9,8},{10,9},{11,1... | collective-permute-start | bytes 196616 | tf_op jit(solution)/shard_map/ppermute | solution.py:15
  42.4 1.3 copy-start.2
  45.6 1.3 copy-start.5
  46.9 1.3 copy-start.4
  49.3 1.3 copy-start.6
  110.7 2.6 collective-permute-start.2
  111.4 7.5 %collective-permute-start.3 = (bf16[1,1,16,16,128]{4,3,2,1,0:T(8,128)(2,1)S(1)}, bf16[1,1,16,16,128]{4,3,2,1,0:T(8,128)(2,1)S(1)}, u32[]{:S(2)}, u32[]{:S(2)}) collective-permute-start(bf16[1,1,16,16,128]{4,3,2,1,0:T(8,128)(2,1)S(1)} %get-tuple-element.112), channel_id=1, source_target_pairs={{0,1},{1,2},{2,3},{3,4},{4,5},{5,6},{6,7},{7,8},{8,9},{9,10},{10,1... | collective-permute-start | bytes 196616 | tf_op jit(solution)/shard_map/ppermute | solution.py:14
  119.3 1.3 copy-start.3
Sparse Core Ops, SparseCore 0:
  112.7 155.0 all-reduce.3
where the time goes:
time: 288 us; the launch traced here: 283 us
  waiting for transfers between devices  144 us (50%)
  matrix products  85.4 us (30%)
  other arithmetic  18.4 us (6%)
  between operations  15.8 us (5%)
  local copies, waits for them, and re-layouts  12.5 us (4%)
  starting transfers between devices  7.38 us (3%)
    unnamed x2, waiting for transfers between devices  138 us
    dot_general x91, matrix products, inner_rows(): lax.dot_general(left_rows, right_rows, (((0,), (0,)), ((), ())), preferre...  67.2 us
    concatenate x67, other arithmetic, window(): piece = jnp.roll(piece, (-shift_y, -shift_x), axis=(2, 3))  11.8 us
    dot_general x27, matrix products, per_device(): lax.dot_general(slope_moved, kernel_weight[offset], (((1,), (1,)), ((), (...  6.89 us
    ppermute x2, starting transfers between devices, padded_2(): after = lax.ppermute(leading, axis, down)  6.61 us
    dot_general x27, matrix products, per_device(): jnp.dot(moved, kernel_weight[offset], preferred_element_type=jnp.float32)  6.55 us
  transfers between devices with their start and end apart: 5, of which 3 were waited for; matrix products, arithmetic and copies ran while one was open for 13% of the time, Pallas kernels for 0%

commit v1 on v0

v1 whole, which is shorter than its diff:
```python
import functools
import math

import jax
import jax.numpy as jnp
from jax import lax
from jax.experimental import pallas as pl
from jax.experimental.pallas import tpu as pltpu
from jax.sharding import PartitionSpec as P

F32 = jnp.float32
BF16 = jnp.bfloat16
TAPS = 27
SIDE = 3
LAGS = 63
GROUP = 8


def vmem():
    return pl.BlockSpec(memory_space=pltpu.VMEM)


def smem():
    return pl.BlockSpec(memory_space=pltpu.SMEM)


def lag_shift(lag):
    number = lag + 62
    return (number // 25 - 2, number // 5 % 5 - 2, number % 5 - 2)


def lag_blocks():
    blocks = []
    for lag in range(LAGS):
        dz, dy, dx = lag_shift(lag)
        key = (dz, dy, dx - dx % 2)
        if key not in blocks:
            blocks.append(key)
    return blocks


def call(kernel, outs, scratch, args, scalars=1, limit=None):
    return pl.pallas_call(
        kernel,
        out_shape=[jax.ShapeDtypeStruct(s, d) for s, d in outs],
        in_specs=[smem()] * scalars + [vmem()] * (len(args) - scalars),
        out_specs=[vmem()] * len(outs),
        scratch_shapes=[pltpu.VMEM(s, d) for s, d in scratch],
        compiler_params=pltpu.CompilerParams(vmem_limit_bytes=limit),
        name=kernel.__name__ if hasattr(kernel, "__name__") else kernel.func.__name__,
    )(*args)


def roll_x(rows, shift, ny, nx):
    cube = rows.reshape(ny, nx, rows.shape[-1])
    shift = shift % nx
    cube = jnp.concatenate([cube[:, nx - shift :], cube[:, : nx - shift]], axis=1)
    return cube.reshape(rows.shape)


def pad_planes(dst, own, low, high):
    depth, ny, nx, chans = own.shape
    plane = ny * nx
    for p in range(depth + 2):
        src = low[0] if p == 0 else high[0] if p == depth + 1 else own[p - 1]
        flat = src.reshape(plane, chans)
        dst[p, nx : nx + plane] = flat
        dst[p, :nx] = flat[plane - nx :]
        dst[p, nx + plane :] = flat[:nx]


def forward_kernel(scale, idx, act, low, high, up, w, actv, slope, keep, send, apad, wcat, s3, at, wg):
    depth, ny, nx, c = act.shape
    plane = ny * nx
    pad_planes(apad, act, low, high)
    for o in range(TAPS):
        q, x = divmod(o, SIDE)
        wcat[q * c : (q + 1) * c, x * c : (x + 1) * c] = w[o]
    for z in range(depth):
        lhs = jnp.concatenate(
            [apad[z + a, b * nx : b * nx + plane] for a in range(SIDE) for b in range(SIDE)], axis=1
        )
        zz = jnp.dot(lhs, wcat[...], preferred_element_type=F32)
        pre = (
            zz[:, c : 2 * c]
            + roll_x(zz[:, :c], 1, ny, nx)
            + roll_x(zz[:, 2 * c :], -1, ny, nx)
        )
        logistic = jax.nn.sigmoid(pre)
        actv[z] = (pre * logistic).astype(BF16).reshape(ny, nx, c)
        grad = (
            up[z].reshape(plane, c).astype(F32) * logistic * (1.0 + pre * (1.0 - logistic))
        ).astype(BF16)
        slope[z] = grad.reshape(ny, nx, c)
        wide = grad.astype(F32)
        rows = slice(z * plane, (z + 1) * plane)
        s3[rows, :c] = roll_x(wide, -1, ny, nx).astype(BF16)
        s3[rows, c : 2 * c] = grad
        s3[rows, 2 * c :] = roll_x(wide, 1, ny, nx).astype(BF16)
    for p in range(depth + 2):
        for b in range(SIDE):
            at[b, :, p * plane : (p + 1) * plane] = apad[p, b * nx : b * nx + plane].T
    for a in range(SIDE):
        for b in range(SIDE):
            lhs = at[b, :, a * plane : (a + depth) * plane]
            out = jnp.dot(lhs, s3[...], preferred_element_type=F32) * scale
            for x in range(SIDE):
                o = (a * SIDE + b) * SIDE + x
                wg[o * c : (o + 1) * c] = out[:, x * c : (x + 1) * c]
    middle = s3[:, c : 2 * c]
    wg[TAPS * c :] = jnp.dot(middle.T, middle, preferred_element_type=F32) * scale
    half = wg.shape[0] // 2
    core = idx[0] & 1
    keep[...] = wg[pl.ds(pl.multiple_of(core * half, 8), half)]
    send[...] = wg[pl.ds(pl.multiple_of((1 - core) * half, 8), half)]


def back_kernel(own, low, high, w, out, spad, wt):
    depth, ny, nx, c = own.shape
    plane = ny * nx
    pad_planes(spad, own, low, high)
    for o in range(TAPS):
        q, x = divmod(o, SIDE)
        wt[x * c : (x + 1) * c, q * c : (q + 1) * c] = w[o]
    for z in range(depth):
        lhs = jnp.concatenate(
            [
                spad[z + 2 - a, (2 - b) * nx : (2 - b) * nx + plane]
                for a in range(SIDE)
                for b in range(SIDE)
            ],
            axis=1,
        )
        zz = lax.dot_general(lhs, wt[...], (((1,), (1,)), ((), ())), preferred_element_type=F32)
        total = (
            zz[:, c : 2 * c]
            + roll_x(zz[:, :c], -1, ny, nx)
            + roll_x(zz[:, 2 * c :], 1, ny, nx)
        )
        out[z] = total.astype(BF16).reshape(ny, nx, c)


def split_kernel(idx, kept, got, *outs):
    quarters = len(outs)
    rows = outs[0].shape[0]
    here = (idx[0] // 2) % quarters
    for k in range(quarters):
        at = pl.ds(pl.multiple_of((here ^ k) * rows, 8), rows)
        outs[k][...] = kept[at] + got[at]


def layer_kernel(group, quarters, idx, *refs):
    parts, outs = refs[:quarters], refs[quarters:-1]
    total = refs[-1]
    value = parts[0][...]
    for part in parts[1:]:
        value = value + part[...]
    total[...] = value
    rows = outs[0].shape[0]
    here = idx[0] // group
    for k in range(len(outs)):
        outs[k][...] = total[pl.ds(pl.multiple_of((here ^ k) * rows, 8), rows)]


def lag_kernel(group, scale, own, idx, low, sel, *refs):
    slabs, rest = refs[:group], refs[group:]
    outs, (af, lhs, right, acc) = rest[:-4], rest[-4:]
    depth, ny, nx, c = slabs[0].shape
    plane = ny * nx
    cells = depth * plane
    count = sel.shape[0]
    blocks = lag_blocks()
    here = idx[0] & (group - 1)
    nt = (((1,), (1,)), ((), ()))
    af[:, : 2 * plane] = lax.dot_general(
        sel[...], low[...].reshape(2 * plane, c), nt, preferred_element_type=F32
    )
    for r in range(group):
        at = here ^ r
        flat = slabs[r][...].reshape(cells, c)
        af[:, pl.ds(pl.multiple_of(2 * plane + at * cells, 128), cells)] = lax.dot_general(
            sel[...], flat, nt, preferred_element_type=F32
        )
        rows = pl.ds(pl.multiple_of(at * cells, 16), cells)
        right[rows, :c] = flat
        right[rows, c:] = roll_x(flat.astype(F32), -1, depth * ny, nx).astype(BF16)
    column = lax.broadcasted_iota(jnp.int32, (count, plane), 1) % nx

    def fill(p, carry):
        base = af[:, pl.ds(pl.multiple_of(p * plane, 128), plane)]
        for dxb in (-2, 0, 2):
            moved = base
            if dxb > 0:
                moved = jnp.where(
                    column < dxb,
                    pltpu.roll(base, (dxb - nx) % plane, 1),
                    pltpu.roll(base, dxb, 1),
                )
            elif dxb < 0:
                moved = jnp.where(
                    column >= nx + dxb,
                    pltpu.roll(base, nx + dxb, 1),
                    pltpu.roll(base, dxb % plane, 1),
                )
            for dy in range(-2, 3):
                tile = (moved if dy == 0 else pltpu.roll(moved, (nx * dy) % plane, 1)).astype(BF16)
                for dz in range(3):
                    if (dz, dy, dxb) in blocks:
                        b = blocks.index((dz, dy, dxb))
                        lhs[b * count : (b + 1) * count, pl.ds(pl.multiple_of((p + dz) * plane, 128), plane)] = tile
        return carry

    lax.fori_loop(0, group * depth + 2, fill, 0)
    acc[...] = jnp.zeros_like(acc)

    def multiply(s, carry):
        left = lhs[:, pl.ds(pl.multiple_of(2 * plane + s * cells, 128), cells)]
        acc[...] += jnp.dot(
            left, right[pl.ds(pl.multiple_of(s * cells, 16), cells)], preferred_element_type=F32
        )
        return carry

    lax.fori_loop(0, group, multiply, 0)
    for out in outs:
        out[LAGS * own :] = jnp.zeros((out.shape[0] - LAGS * own, c), F32)
    for lag in range(LAGS):
        dz, dy, dx = lag_shift(lag)
        odd = dx % 2
        b = blocks.index((dz, dy, dx - odd))
        for k, out in enumerate(outs):
            start = b * count + k * own
            out[lag * own : (lag + 1) * own] = (
                acc[start : start + own, odd * c : (odd + 1) * c] * scale
            )


def factor_kernel(*refs):
    parts, out, total = refs[:-2], refs[-2], refs[-1]
    value = parts[0][...]
    for part in parts[1:]:
        value = value + part[...]
    total[...] = value
    own = out.shape[0]
    for j in range(own):
        out[j] = total[pl.ds(j, LAGS, stride=own)]


def halve_kernel(inverse, out, flat):
    taps, own, patch = inverse.shape
    rows = out.shape[0] // 2
    flat[taps * own :] = jnp.zeros((rows - taps * own, patch), F32)
    for o in range(taps):
        flat[o * own : (o + 1) * own] = inverse[o]
    value = flat[...]
    upper = value.astype(BF16)
    out[:rows] = upper
    out[rows:] = (value - upper.astype(F32)).astype(BF16)


def precond_kernel(group, layers, idx, halves, q, *refs):
    quarters = group // 2
    parts = refs[:group]
    out, factor, w = refs[group:]
    taps, own, c = out.shape
    patch = halves.shape[1]
    rows = parts[0].shape[0] // layers
    core = idx[0] & 1
    here = (idx[0] // 2) % quarters
    layer = idx[0] // group
    for r in range(group):
        k, other = divmod(r, 2)
        for m in range(layers):
            block = ((core ^ other) * quarters + (here ^ k)) * layers + (layer ^ m)
            w[pl.ds(pl.multiple_of(block * rows, 8), rows)] = parts[r][m * rows : (m + 1) * rows]
    factor[...] = w[patch:]
    value = w[:patch]
    upper = value.astype(BF16)
    both = jnp.concatenate([upper, (value - upper.astype(F32)).astype(BF16)], axis=1)
    product = jnp.dot(halves[...], both, preferred_element_type=F32)
    n = halves.shape[0] // 2
    left = (product[n:, :c] + product[:n, c:]) + product[n:, c:] + product[:n, :c]
    result = jnp.dot(left, q[...], precision=lax.Precision.HIGHEST, preferred_element_type=F32)
    for o in range(taps):
        out[o] = result[o * own : (o + 1) * own]


def per_device(activations, upstream, kernel_weight, patch_inverse, output_inverse):
    n = lax.axis_size("space")
    dp = lax.axis_size("dp")
    group = math.gcd(n, GROUP)
    quarters = group // 2
    layers = n // group
    _, depth, ny, nx, c = activations.shape
    plane = ny * nx
    cells = depth * plane
    own = patch_inverse.shape[1]
    patch = patch_inverse.shape[2]
    scale = 1.0 / float(cells * n * dp)
    me = lax.axis_index("space").astype(jnp.int32)
    idx = me.reshape(1)

    def flip(x, bits):
        return lax.ppermute(x, "space", [(i, i ^ bits) for i in range(n)])

    def shift(x, by):
        return lax.ppermute(x, "space", [(i, (i + by) % n) for i in range(n)])

    act = activations[0]
    up = upstream[0]
    low = shift(act[depth - 1 :], 1)
    high = shift(act[:1], -1)
    side = [act] + [flip(act, 2 * k) for k in range(1, quarters)]
    slabs = []
    for part in side:
        slabs += [part, flip(part, 1)]

    rows = (TAPS + 1) * c
    pad = (depth + 2, plane + 2 * nx, c)
    forward = functools.partial(forward_kernel, scale)
    actv, slope, keep, send = call(
        forward,
        [(act.shape, BF16), (act.shape, BF16), ((rows // 2, c), F32), ((rows // 2, c), F32)],
        [
            (pad, BF16),
            ((9 * c, 3 * c), BF16),
            ((cells, 3 * c), BF16),
            ((SIDE, c, (depth + 2) * plane), BF16),
            ((rows, c), F32),
        ],
        (idx, act, low, high, up, kernel_weight),
    )
    got = flip(send, 1)
    slope_low = shift(slope[depth - 1 :], 1)
    slope_high = shift(slope[:1], -1)
    piece = rows // group
    quarter = call(split_kernel, [((piece, c), F32)] * quarters, [], (idx, keep, got))
    quarter = [quarter[0]] + [flip(quarter[k], 2 * k) for k in range(1, quarters)]

    last = lax.select_n(
        (me % group) ^ (group - 1), *[slab[depth - 2 :] for slab in slabs]
    )
    below = shift(last, group)
    number = jnp.arange(layers * own, dtype=jnp.int32)
    layer = number // own ^ me // group
    channel = (layer * group + me % group) * own + number % own
    sel = (channel[:, None] == jnp.arange(c, dtype=jnp.int32)[None, :]).astype(BF16)
    count = layers * own
    nblocks = len(lag_blocks())
    lag_rows = -(-LAGS * own // 8) * 8
    lag = functools.partial(lag_kernel, group, scale, own)
    partial = call(
        lag,
        [((lag_rows, c), F32)] * layers,
        [
            ((count, (group * depth + 2) * plane), F32),
            ((nblocks * count, (group * depth + 4) * plane), BF16),
            ((group * cells, 2 * c), BF16),
            ((nblocks * count, 2 * c), F32),
        ],
        (idx, below, sel, *slabs),
        limit=50 << 20,
    )

    (input_grad,) = call(
        back_kernel,
        [(act.shape, BF16)],
        [(pad, BF16), ((3 * c, 9 * c), BF16)],
        (slope, slope_low, slope_high, kernel_weight),
        scalars=0,
    )

    thin = piece // layers
    layered = functools.partial(layer_kernel, group, quarters)
    pieces = call(
        layered, [((thin, c), F32)] * layers, [((piece, c), F32)], (idx, *quarter)
    )
    mine = pieces[0]
    for k in range(1, layers):
        mine = mine + flip(pieces[k], k * group)
    if dp > 1:
        mine = lax.psum(mine, "dp")
    column = jnp.concatenate([mine] + [flip(mine, k * group) for k in range(1, layers)], axis=0)
    whole = []
    for k in range(quarters):
        part = column if k == 0 else flip(column, 2 * k)
        whole += [part, flip(part, 1)]

    lag_parts = [partial[0]] + [flip(partial[k], k * group) for k in range(1, layers)]
    (patch_factor,) = call(
        factor_kernel, [((own, LAGS, c), F32)], [((lag_rows, c), F32)], tuple(lag_parts), scalars=0
    )
    if dp > 1:
        patch_factor = lax.psum_scatter(patch_factor, "dp", scatter_dimension=2, tiled=True)

    half_rows = -(-TAPS * own // 16) * 16
    (halves,) = call(
        halve_kernel, [((2 * half_rows, patch), BF16)], [((half_rows, patch), F32)], (patch_inverse,), scalars=0
    )
    precond = functools.partial(precond_kernel, group, layers)
    precond_grad, output_factor = call(
        precond,
        [((TAPS, own, c), F32), ((c, c), F32)],
        [((rows, c), F32)],
        (idx, halves, output_inverse, *whole),
    )
    return (actv[None], input_grad[None], patch_factor, output_factor, precond_grad)


def solution(mesh):
    return jax.shard_map(
        per_device,
        mesh=mesh,
        in_specs=(
            P("dp", "space", None, None, None),
            P("dp", "space", None, None, None),
            P(),
            P(None, "space", None),
            P(),
        ),
        out_specs=(
            P("dp", "space", None, None, None),
            P("dp", "space", None, None, None),
            P("space", None, "dp"),
            P(),
            P(None, "space", None),
        ),
        check_vma=False,
    )
```

time: 288 us -> 117 us (0.41); the launches traced: 283 us -> 117 us
  waiting for transfers between devices: 144 us -> 36.7 us
  matrix products: 85.4 us -> 0 us
  Pallas kernels: 0 us -> 33.7 us
  starting transfers between devices: 7.38 us -> 36.7 us
  other arithmetic: 18.4 us -> 0.98 us
  between operations: 15.8 us -> 0.87 us
  local copies, waits for them, and re-layouts: 12.5 us -> 7.7 us
    unnamed x2 -> x0, waiting for transfers between devices: 138 us -> none
    dot_general x147 -> x0, matrix products: 85.4 us -> none  [the longest x91 67.2 us: inner_rows(): lax.dot_general(left_rows, right_rows, (((0,), (0,)), ((), ())), preferre...]
    pallas_call x0 -> x8, Pallas kernels: none -> 33.7 us  [call(): pl.pallas_call(kernel, out_shape=[jax.ShapeDtypeStruct(s, d) for s, d in...]
    ppermute x4 -> x32, waiting for transfers between devices: 6.35 us -> 36.7 us  [the longest x27 32.8 us: flip(): return lax.ppermute(x, 'space', [(i, i ^ bits) for i in range(n)])]
    ppermute x4 -> x32, starting transfers between devices: 7.34 us -> 36.7 us  [the longest x27 28.9 us: flip(): return lax.ppermute(x, 'space', [(i, i ^ bits) for i in range(n)])]
    concatenate x71 -> x1, other arithmetic: 12.3 us -> 0.02 us  [per_device(): jnp.concatenate([mine] + [flip(mine, k * group) for k in range(1, layers)...]
    div x2 -> x0, other arithmetic: 6.11 us -> none  [the longest x1 4.71 us: per_device(): jnp.stack(blocks, axis=1) / total]
    slice x28 -> x2, local copies, waits for them, and re-layouts: 4.78 us -> 0.89 us  [the longest x1 0.88 us: per_device(): high = shift(act[:1], -1)]
  transfers between devices with their start and end apart: 5 -> 32, of which waited for: 3 -> 11; matrix products, arithmetic and copies ran while one was open for 13% -> 2% of each run, Pallas kernels for 0% -> 18%
where the time goes in v1:
time: 117 us
  starting transfers between devices  36.7 us (31%)
  waiting for transfers between devices  36.7 us (31%)
  Pallas kernels  33.7 us (29%)
  local copies, waits for them, and re-layouts  7.7 us (7%)
    pallas_call x8, Pallas kernels, call(): pl.pallas_call(kernel, out_shape=[jax.ShapeDtypeStruct(s, d) for s, d in...  33.7 us
    ppermute x27, waiting for transfers between devices, flip(): return lax.ppermute(x, 'space', [(i, i ^ bits) for i in range(n)])  32.8 us
    ppermute x27, starting transfers between devices, flip(): return lax.ppermute(x, 'space', [(i, i ^ bits) for i in range(n)])  28.9 us
    ppermute x5, starting transfers between devices, shift(): return lax.ppermute(x, 'space', [(i, (i + by) % n) for i in range(n)])  7.86 us
    unnamed x45, local copies, waits for them, and re-layouts  6.8 us
    ppermute x5, waiting for transfers between devices, shift(): return lax.ppermute(x, 'space', [(i, (i + by) % n) for i in range(n)])  3.9 us
  transfers between devices with their start and end apart: 32, of which 11 were waited for; matrix products, arithmetic and copies ran while one was open for 2% of the time, Pallas kernels for 18%

profile of v1, /device:TPU:0, one launch (start us, length us, event | category | flops | bytes accessed | tf_op | source)
XLA Modules:
  0.0 116.7 jit_solution(11648721249736975793)
XLA Ops:
  2.1 6.0 %collective-permute-start.1 = (bf16[1,16,16,128]{3,2,1,0:T(8,128)(2,1)S(1)}, bf16[1,16,16,128]{3,2,1,0:T(8,128)(2,1)S(1)}, u32[]{:S(2)}, u32[]{:S(2)}) collective-permute-start(bf16[1,16,16,128]{3,2,1,0:T(8,128)(2,1)S(1)} %get-tuple-element.48), channel_id=1, source_target_pairs={{0,31},{1,0},{2,1},{3,2},{4,3},{5,4},{6,5},{7,6},{8,7},{9,8},{10,9... | collective-permute-start | bytes 196616 | tf_op jit(solution)/shard_map/ppermute | solution.py:306
  8.0 2.0 %collective-permute-done.low = bf16[1,16,16,128]{3,2,1,0:T(8,128)(2,1)S(1)} collective-permute-done((bf16[1,16,16,128]{3,2,1,0:T(8,128)(2,1)S(1)}, bf16[1,16,16,128]{3,2,1,0:T(8,128)(2,1)S(1)}, u32[]{:S(2)}, u32[]{:S(2)}) %collective-permute-start) | collective-permute-done | bytes 65568 | tf_op jit(solution)/shard_map/ppermute | solution.py:306
  10.7 6.2 %forward_kernel.1 = (bf16[4,16,16,128]{3,2,1,0:T(8,128)(2,1)}, bf16[4,16,16,128]{3,2,1,0:T(8,128)(2,1)}, f32[1792,128]{1,0:T(8,128)}, f32[1792,128]{1,0:T(8,128)}) custom-call(s32[1]{0:T(128)} %bitcast.idx, bf16[4,16,16,128]{3,2,1,0:T(8,128)(2,1)} %bitcast.11, bf16[1,16,16,128]{3,2,1,0:T(8,128)(2,1)} %copy-done.20, bf16[1,16,16,128]{3,2,1,0:T(8,128)(2,1)} %copy-done.21, ...), custom_call_target="tpu_custom_call" | custom-call | tf_op jit(solution)/shard_map/forward_kernel/pallas_call | solution.py:43
  16.9 2.7 %collective-permute-done.15.got = f32[1792,128]{1,0:T(8,128)S(1)} collective-permute-done((f32[1792,128]{1,0:T(8,128)}, f32[1792,128]{1,0:T(8,128)S(1)}, u32[]{:S(2)}, u32[]{:S(2)}) %collective-permute-start.15) | collective-permute-done | bytes 917536 | tf_op jit(solution)/shard_map/ppermute | solution.py:303
  20.5 2.5 %split_kernel.1 = (f32[448,128]{1,0:T(8,128)}, f32[448,128]{1,0:T(8,128)}, f32[448,128]{1,0:T(8,128)}, f32[448,128]{1,0:T(8,128)}) custom-call(s32[1]{0:T(128)} %bitcast.idx, f32[1792,128]{1,0:T(8,128)} %get-tuple-element.29.kept, f32[1792,128]{1,0:T(8,128)} %copy-done.3), custom_call_target="tpu_custom_call" | custom-call | tf_op jit(solution)/shard_map/split_kernel/pallas_call | solution.py:43
  23.3 2.4 %collective-permute-start.17 = (f32[448,128]{1,0:T(8,128)}, f32[448,128]{1,0:T(8,128)S(1)}, u32[]{:S(2)}, u32[]{:S(2)}) collective-permute-start(f32[448,128]{1,0:T(8,128)} %get-tuple-element.33), channel_id=1, source_target_pairs={{0,4},{1,5},{2,6},{3,7},{4,0},{5,1},{6,2},{7,3},{8,12},{9,13},{10,... | collective-permute-start | bytes 688136 | tf_op jit(solution)/shard_map/ppermute | solution.py:303
  26.5 2.2 %collective-permute-start.9 = (bf16[4,16,16,128]{3,2,1,0:T(8,128)(2,1)S(1)}, bf16[4,16,16,128]{3,2,1,0:T(8,128)(2,1)S(1)}, u32[]{:S(2)}, u32[]{:S(2)}) collective-permute-start(bf16[4,16,16,128]{3,2,1,0:T(8,128)(2,1)S(1)} %bitcast.12), channel_id=1, source_target_pairs={{0,6},{1,7},{2,4},{3,5},{4,2},{5,3},{6,0},{7,1},{8,14},{9,15},{10,... | collective-permute-start | bytes 786440 | tf_op jit(solution)/shard_map/ppermute | solution.py:303
  28.6 3.0 %collective-permute-done.16.refs_1_ = f32[448,128]{1,0:T(8,128)S(1)} collective-permute-done((f32[448,128]{1,0:T(8,128)}, f32[448,128]{1,0:T(8,128)S(1)}, u32[]{:S(2)}, u32[]{:S(2)}) %collective-permute-start.16) | collective-permute-done | bytes 229408 | tf_op jit(solution)/shard_map/ppermute | solution.py:303
  32.4 10.2 %collective-permute-done.17.refs_2_ = f32[448,128]{1,0:T(8,128)S(1)} collective-permute-done((f32[448,128]{1,0:T(8,128)}, f32[448,128]{1,0:T(8,128)S(1)}, u32[]{:S(2)}, u32[]{:S(2)}) %collective-permute-start.17) | collective-permute-done | bytes 229408 | tf_op jit(solution)/shard_map/ppermute | solution.py:303
  43.3 2.0 %layer_kernel.1 = (f32[112,128]{1,0:T(8,128)}, f32[112,128]{1,0:T(8,128)}, f32[112,128]{1,0:T(8,128)}, f32[112,128]{1,0:T(8,128)}) custom-call(s32[1]{0:T(128)} %bitcast.idx, f32[448,128]{1,0:T(8,128)} %get-tuple-element.31.refs_0_, f32[448,128]{1,0:T(8,128)} %copy-done.12, f32[448,128]{1,0:T(8,128)} %copy-done.13, f32[448,128]{1,0:T(8,128)} %copy-done.14), custom_call_target="tpu_custom_call" | custom-call | tf_op jit(solution)/shard_map/layer_kernel/pallas_call | solution.py:43
  45.3 1.6 %collective-permute-start.19 = (f32[112,128]{1,0:T(8,128)}, f32[112,128]{1,0:T(8,128)S(1)}, u32[]{:S(2)}, u32[]{:S(2)}) collective-permute-start(f32[112,128]{1,0:T(8,128)} %get-tuple-element.36), channel_id=1, source_target_pairs={{0,8},{1,9},{2,10},{3,11},{4,12},{5,13},{6,14},{7,15},{8,0},{9,1},... | collective-permute-start | bytes 172040 | tf_op jit(solution)/shard_map/ppermute | solution.py:303
  46.9 2.7 %collective-permute-start.20 = (f32[112,128]{1,0:T(8,128)}, f32[112,128]{1,0:T(8,128)S(1)}, u32[]{:S(2)}, u32[]{:S(2)}) collective-permute-start(f32[112,128]{1,0:T(8,128)} %get-tuple-element.37), channel_id=1, source_target_pairs={{0,16},{1,17},{2,18},{3,19},{4,20},{5,21},{6,22},{7,23},{8,24},{9,... | collective-permute-start | bytes 172040 | tf_op jit(solution)/shard_map/ppermute | solution.py:303
  50.7 2.1 %collective-permute-done.20 = f32[112,128]{1,0:T(8,128)S(1)} collective-permute-done((f32[112,128]{1,0:T(8,128)}, f32[112,128]{1,0:T(8,128)S(1)}, u32[]{:S(2)}, u32[]{:S(2)}) %collective-permute-start.20) | collective-permute-done | bytes 57376 | tf_op jit(solution)/shard_map/ppermute | solution.py:303
  52.8 1.9 %collective-permute-start.21 = (f32[112,128]{1,0:T(8,128)}, f32[112,128]{1,0:T(8,128)S(1)}, u32[]{:S(2)}, u32[]{:S(2)}) collective-permute-start(f32[112,128]{1,0:T(8,128)} %get-tuple-element.38), channel_id=1, source_target_pairs={{0,24},{1,25},{2,26},{3,27},{4,28},{5,29},{6,30},{7,31},{8,16},{9,... | collective-permute-start | bytes 172040 | tf_op jit(solution)/shard_map/ppermute | solution.py:303
  54.7 4.3 %collective-permute-done.21 = f32[112,128]{1,0:T(8,128)S(1)} collective-permute-done((f32[112,128]{1,0:T(8,128)}, f32[112,128]{1,0:T(8,128)S(1)}, u32[]{:S(2)}, u32[]{:S(2)}) %collective-permute-start.21) | collective-permute-done | bytes 57376 | tf_op jit(solution)/shard_map/ppermute | solution.py:303
  59.9 2.4 %collective-permute-start.23 = (f32[112,128]{1,0:T(8,128)S(1)}, f32[112,128]{1,0:T(8,128)S(1)}, u32[]{:S(2)}, u32[]{:S(2)}) collective-permute-start(f32[112,128]{1,0:T(8,128)S(1)} %add_add_fusion), channel_id=1, source_target_pairs={{0,16},{1,17},{2,18},{3,19},{4,20},{5,21},{6,22},{7,23},{8,24},{9,... | collective-permute-start | bytes 172040 | tf_op jit(solution)/shard_map/ppermute | solution.py:303
  62.4 2.0 %collective-permute-start.24 = (f32[112,128]{1,0:T(8,128)S(1)}, f32[112,128]{1,0:T(8,128)S(1)}, u32[]{:S(2)}, u32[]{:S(2)}) collective-permute-start(f32[112,128]{1,0:T(8,128)S(1)} %add_add_fusion), channel_id=1, source_target_pairs={{0,24},{1,25},{2,26},{3,27},{4,28},{5,29},{6,30},{7,31},{8,16},{9,... | collective-permute-start | bytes 172040 | tf_op jit(solution)/shard_map/ppermute | solution.py:303
  64.9 2.5 %collective-permute-done.23 = f32[112,128]{1,0:T(8,128)S(1)} collective-permute-done((f32[112,128]{1,0:T(8,128)S(1)}, f32[112,128]{1,0:T(8,128)S(1)}, u32[]{:S(2)}, u32[]{:S(2)}) %collective-permute-start.23) | collective-permute-done | bytes 57376 | tf_op jit(solution)/shard_map/ppermute | solution.py:303
  67.4 1.3 %collective-permute-done.24 = f32[112,128]{1,0:T(8,128)S(1)} collective-permute-done((f32[112,128]{1,0:T(8,128)S(1)}, f32[112,128]{1,0:T(8,128)S(1)}, u32[]{:S(2)}, u32[]{:S(2)}) %collective-permute-start.24) | collective-permute-done | bytes 57376 | tf_op jit(solution)/shard_map/ppermute | solution.py:303
  68.8 2.4 %collective-permute-start.28 = (f32[448,128]{1,0:T(8,128)S(1)}, f32[448,128]{1,0:T(8,128)S(1)}, u32[]{:S(2)}, u32[]{:S(2)}) collective-permute-start(f32[448,128]{1,0:T(8,128)S(1)} %pad_maximum_fusion.refs_0_), channel_id=1, source_target_pairs={{0,4},{1,5},{2,6},{3,7},{4,0},{5,1},{6,2},{7,3},{8,12},{9,13},{10,... | collective-permute-start | bytes 688136 | tf_op jit(solution)/shard_map/ppermute | solution.py:303
  71.2 1.4 %collective-permute-start.30 = (f32[448,128]{1,0:T(8,128)S(1)}, f32[448,128]{1,0:T(8,128)S(1)}, u32[]{:S(2)}, u32[]{:S(2)}) collective-permute-start(f32[448,128]{1,0:T(8,128)S(1)} %pad_maximum_fusion.refs_0_), channel_id=1, source_target_pairs={{0,6},{1,7},{2,4},{3,5},{4,2},{5,3},{6,0},{7,1},{8,14},{9,15},{10,... | collective-permute-start | bytes 688136 | tf_op jit(solution)/shard_map/ppermute | solution.py:303
  72.7 11.1 %lag_kernel.1 = (f32[256,128]{1,0:T(8,128)S(1)}, f32[256,128]{1,0:T(8,128)S(1)}, f32[256,128]{1,0:T(8,128)S(1)}, f32[256,128]{1,0:T(8,128)S(1)}) custom-call(s32[1]{0:T(128)} %bitcast.idx, bf16[2,16,16,128]{3,2,1,0:T(8,128)(2,1)S(1)} %collective-permute-done.11.low, bf16[16,128]{1,0:T(8,128)(2,1)S(1)} %fusion.3.sel, bf16[4,16,16,128]{3,2,1,0:T(8,128)(2,1)S(1)} %bitcast.16, ...), custom_call_target="tpu_custom_call" | custom-call | tf_op jit(solution)/shard_map/lag_kernel/pallas_call | solution.py:43
  84.4 3.3 %collective-permute-start.12 = (f32[256,128]{1,0:T(8,128)S(1)}, f32[256,128]{1,0:T(8,128)S(1)}, u32[]{:S(2)}, u32[]{:S(2)}) collective-permute-start(f32[256,128]{1,0:T(8,128)S(1)} %get-tuple-element.26), channel_id=1, source_target_pairs={{0,8},{1,9},{2,10},{3,11},{4,12},{5,13},{6,14},{7,15},{8,0},{9,1},... | collective-permute-start | bytes 393224 | tf_op jit(solution)/shard_map/ppermute | solution.py:303
  87.7 1.3 %collective-permute-start.3 = (bf16[1,16,16,128]{3,2,1,0:T(8,128)(2,1)S(1)}, bf16[1,16,16,128]{3,2,1,0:T(8,128)(2,1)S(1)}, u32[]{:S(2)}, u32[]{:S(2)}) collective-permute-start(bf16[1,16,16,128]{3,2,1,0:T(8,128)(2,1)S(1)} %get-tuple-element.46), channel_id=1, source_target_pairs={{0,31},{1,0},{2,1},{3,2},{4,3},{5,4},{6,5},{7,6},{8,7},{9,8},{10,9... | collective-permute-start | bytes 196616 | tf_op jit(solution)/shard_map/ppermute | solution.py:306
  89.0 1.9 %collective-permute-done.3.high = bf16[1,16,16,128]{3,2,1,0:T(8,128)(2,1)S(1)} collective-permute-done((bf16[1,16,16,128]{3,2,1,0:T(8,128)(2,1)S(1)}, bf16[1,16,16,128]{3,2,1,0:T(8,128)(2,1)S(1)}, u32[]{:S(2)}, u32[]{:S(2)}) %collective-permute-start.3) | collective-permute-done | bytes 65568 | tf_op jit(solution)/shard_map/ppermute | solution.py:306
  93.0 6.2 %collective-permute-done.13.refs_2_ = f32[256,128]{1,0:T(8,128)S(1)} collective-permute-done((f32[256,128]{1,0:T(8,128)S(1)}, f32[256,128]{1,0:T(8,128)S(1)}, u32[]{:S(2)}, u32[]{:S(2)}) %collective-permute-start.13) | collective-permute-done | bytes 131104 | tf_op jit(solution)/shard_map/ppermute | solution.py:303
  99.2 1.6 %collective-permute-start.14 = (f32[256,128]{1,0:T(8,128)S(1)}, f32[256,128]{1,0:T(8,128)S(1)}, u32[]{:S(2)}, u32[]{:S(2)}) collective-permute-start(f32[256,128]{1,0:T(8,128)S(1)} %get-tuple-element.28), channel_id=1, source_target_pairs={{0,24},{1,25},{2,26},{3,27},{4,28},{5,29},{6,30},{7,31},{8,16},{9,... | collective-permute-start | bytes 393224 | tf_op jit(solution)/shard_map/ppermute | solution.py:303
  100.8 3.1 %halve_kernel.1.halves = bf16[224,3456]{1,0:T(8,128)(2,1)} custom-call(f32[27,4,3456]{2,1,0:T(4,128)} %inverse.1), custom_call_target="tpu_custom_call" | custom-call | tf_op jit(solution)/shard_map/halve_kernel/pallas_call | solution.py:43
  103.9 3.6 %back_kernel.1 = bf16[4,16,16,128]{3,2,1,0:T(8,128)(2,1)} custom-call(bf16[4,16,16,128]{3,2,1,0:T(8,128)(2,1)} %get-tuple-element.24.own, bf16[1,16,16,128]{3,2,1,0:T(8,128)(2,1)} %copy-done.18, bf16[1,16,16,128]{3,2,1,0:T(8,128)(2,1)} %copy-done.19, bf16[27,128,128]{2,1,0:T(8,128)(2,1)} %w.3), custom_call_target="tpu_custom_call" | custom-call | tf_op jit(solution)/shard_map/back_kernel/pallas_call | solution.py:43
  108.1 1.8 %factor_kernel.1 = f32[4,63,128]{2,1,0:T(8,128)} custom-call(f32[256,128]{1,0:T(8,128)} %copy-done.1, f32[256,128]{1,0:T(8,128)} %copy-done.15, f32[256,128]{1,0:T(8,128)} %copy-done.16, f32[256,128]{1,0:T(8,128)} %copy-done.17), custom_call_target="tpu_custom_call" | custom-call | tf_op jit(solution)/shard_map/factor_kernel/pallas_call | solution.py:43
  109.9 1.6 %copy.10 = f32[4,63,128]{2,0,1:T(4,128)} copy(f32[4,63,128]{2,1,0:T(8,128)} %factor_kernel.1) | data formatting | bytes 258048
  113.1 3.6 %precond_kernel.1 = (f32[27,4,128]{2,1,0:T(4,128)}, f32[128,128]{1,0:T(8,128)}) custom-call(s32[1]{0:T(128)} %bitcast.idx, bf16[224,3456]{1,0:T(8,128)(2,1)} %halve_kernel.1.halves, f32[128,128]{1,0:T(8,128)} %q.1, f32[448,128]{1,0:T(8,128)} %copy-done.2, f32[448,128]{1,0:T(8,128)} %copy-done.8, f32[448,128]{1,0:T(8,128)} %copy-done.5, ...), custom_call_target="tpu_custom_call" | custom-call | tf_op jit(solution)/shard_map/precond_kernel/pallas_call | solution.py:43
  (92 shorter events, 13.2 us)
Async XLA Ops:
  1.5 8.5 %collective-permute-start = (bf16[1,16,16,128]{3,2,1,0:T(8,128)(2,1)S(1)}, bf16[1,16,16,128]{3,2,1,0:T(8,128)(2,1)S(1)}, u32[]{:S(2)}, u32[]{:S(2)}) collective-permute-start(bf16[1,16,16,128]{3,2,1,0:T(8,128)(2,1)S(1)} %get-tuple-element.49), channel_id=1, source_target_pairs={{0,1},{1,2},{2,3},{3,4},{4,5},{5,6},{6,7},{7,8},{8,9},{9,10},{10,1... | collective-permute-start | bytes 196616 | tf_op jit(solution)/shard_map/ppermute | solution.py:306
  2.1 8.0 %collective-permute-start.1 = (bf16[1,16,16,128]{3,2,1,0:T(8,128)(2,1)S(1)}, bf16[1,16,16,128]{3,2,1,0:T(8,128)(2,1)S(1)}, u32[]{:S(2)}, u32[]{:S(2)}) collective-permute-start(bf16[1,16,16,128]{3,2,1,0:T(8,128)(2,1)S(1)} %get-tuple-element.48), channel_id=1, source_target_pairs={{0,31},{1,0},{2,1},{3,2},{4,3},{5,4},{6,5},{7,6},{8,7},{9,8},{10,9... | collective-permute-start | bytes 196616 | tf_op jit(solution)/shard_map/ppermute | solution.py:306
  16.9 2.7 %collective-permute-start.15 = (f32[1792,128]{1,0:T(8,128)}, f32[1792,128]{1,0:T(8,128)S(1)}, u32[]{:S(2)}, u32[]{:S(2)}) collective-permute-start(f32[1792,128]{1,0:T(8,128)} %get-tuple-element.30), channel_id=1, source_target_pairs={{0,1},{1,0},{2,3},{3,2},{4,5},{5,4},{6,7},{7,6},{8,9},{9,8},{10,11... | collective-permute-start | bytes 2752520 | tf_op jit(solution)/shard_map/ppermute | solution.py:303
  23.0 8.7 %collective-permute-start.16 = (f32[448,128]{1,0:T(8,128)}, f32[448,128]{1,0:T(8,128)S(1)}, u32[]{:S(2)}, u32[]{:S(2)}) collective-permute-start(f32[448,128]{1,0:T(8,128)} %get-tuple-element.32), channel_id=1, source_target_pairs={{0,2},{1,3},{2,0},{3,1},{4,6},{5,7},{6,4},{7,5},{8,10},{9,11},{10,... | collective-permute-start | bytes 688136 | tf_op jit(solution)/shard_map/ppermute | solution.py:303
  23.3 19.3 %collective-permute-start.17 = (f32[448,128]{1,0:T(8,128)}, f32[448,128]{1,0:T(8,128)S(1)}, u32[]{:S(2)}, u32[]{:S(2)}) collective-permute-start(f32[448,128]{1,0:T(8,128)} %get-tuple-element.33), channel_id=1, source_target_pairs={{0,4},{1,5},{2,6},{3,7},{4,0},{5,1},{6,2},{7,3},{8,12},{9,13},{10,... | collective-permute-start | bytes 688136 | tf_op jit(solution)/shard_map/ppermute | solution.py:303
  25.7 16.8 %collective-permute-start.18 = (f32[448,128]{1,0:T(8,128)}, f32[448,128]{1,0:T(8,128)S(1)}, u32[]{:S(2)}, u32[]{:S(2)}) collective-permute-start(f32[448,128]{1,0:T(8,128)} %get-tuple-element.34), channel_id=1, source_target_pairs={{0,6},{1,7},{2,4},{3,5},{4,2},{5,3},{6,0},{7,1},{8,14},{9,15},{10,... | collective-permute-start | bytes 688136 | tf_op jit(solution)/shard_map/ppermute | solution.py:303
  26.5 23.1 %collective-permute-start.9 = (bf16[4,16,16,128]{3,2,1,0:T(8,128)(2,1)S(1)}, bf16[4,16,16,128]{3,2,1,0:T(8,128)(2,1)S(1)}, u32[]{:S(2)}, u32[]{:S(2)}) collective-permute-start(bf16[4,16,16,128]{3,2,1,0:T(8,128)(2,1)S(1)} %bitcast.12), channel_id=1, source_target_pairs={{0,6},{1,7},{2,4},{3,5},{4,2},{5,3},{6,0},{7,1},{8,14},{9,15},{10,... | collective-permute-start | bytes 786440 | tf_op jit(solution)/shard_map/ppermute | solution.py:303
  28.6 21.1 %collective-permute-start.5 = (bf16[4,16,16,128]{3,2,1,0:T(8,128)(2,1)S(1)}, bf16[4,16,16,128]{3,2,1,0:T(8,128)(2,1)S(1)}, u32[]{:S(2)}, u32[]{:S(2)}) collective-permute-start(bf16[4,16,16,128]{3,2,1,0:T(8,128)(2,1)S(1)} %bitcast.13), channel_id=1, source_target_pairs={{0,2},{1,3},{2,0},{3,1},{4,6},{5,7},{6,4},{7,5},{8,10},{9,11},{10,... | collective-permute-start | bytes 786440 | tf_op jit(solution)/shard_map/ppermute | solution.py:303
  31.7 18.5 %collective-permute-start.7 = (bf16[4,16,16,128]{3,2,1,0:T(8,128)(2,1)S(1)}, bf16[4,16,16,128]{3,2,1,0:T(8,128)(2,1)S(1)}, u32[]{:S(2)}, u32[]{:S(2)}) collective-permute-start(bf16[4,16,16,128]{3,2,1,0:T(8,128)(2,1)S(1)} %bitcast.14), channel_id=1, source_target_pairs={{0,4},{1,5},{2,6},{3,7},{4,0},{5,1},{6,2},{7,3},{8,12},{9,13},{10,... | collective-permute-start | bytes 786440 | tf_op jit(solution)/shard_map/ppermute | solution.py:303
  45.3 4.9 %collective-permute-start.19 = (f32[112,128]{1,0:T(8,128)}, f32[112,128]{1,0:T(8,128)S(1)}, u32[]{:S(2)}, u32[]{:S(2)}) collective-permute-start(f32[112,128]{1,0:T(8,128)} %get-tuple-element.36), channel_id=1, source_target_pairs={{0,8},{1,9},{2,10},{3,11},{4,12},{5,13},{6,14},{7,15},{8,0},{9,1},... | collective-permute-start | bytes 172040 | tf_op jit(solution)/shard_map/ppermute | solution.py:303
  46.9 5.9 %collective-permute-start.20 = (f32[112,128]{1,0:T(8,128)}, f32[112,128]{1,0:T(8,128)S(1)}, u32[]{:S(2)}, u32[]{:S(2)}) collective-permute-start(f32[112,128]{1,0:T(8,128)} %get-tuple-element.37), channel_id=1, source_target_pairs={{0,16},{1,17},{2,18},{3,19},{4,20},{5,21},{6,22},{7,23},{8,24},{9,... | collective-permute-start | bytes 172040 | tf_op jit(solution)/shard_map/ppermute | solution.py:303
  49.6 10.2 %collective-permute-start.4 = (bf16[4,16,16,128]{3,2,1,0:T(8,128)(2,1)S(1)}, bf16[4,16,16,128]{3,2,1,0:T(8,128)(2,1)S(1)}, u32[]{:S(2)}, u32[]{:S(2)}) collective-permute-start(bf16[4,16,16,128]{3,2,1,0:T(8,128)(2,1)S(1)} %bitcast.15), channel_id=1, source_target_pairs={{0,1},{1,0},{2,3},{3,2},{4,5},{5,4},{6,7},{7,6},{8,9},{9,8},{10,11... | collective-permute-start | bytes 786440 | tf_op jit(solution)/shard_map/ppermute | solution.py:303
  49.7 10.2 %collective-permute-start.10 = (bf16[4,16,16,128]{3,2,1,0:T(8,128)(2,1)S(1)}, bf16[4,16,16,128]{3,2,1,0:T(8,128)(2,1)S(1)}, u32[]{:S(2)}, u32[]{:S(2)}) collective-permute-start(bf16[4,16,16,128]{3,2,1,0:T(8,128)(2,1)S(1)} %collective-permute-done.9.refs_6_), channel_id=1, source_target_pairs={{0,1},{1,0},{2,3},{3,2},{4,5},{5,4},{6,7},{7,6},{8,9},{9,8},{10,11... | collective-permute-start | bytes 786440 | tf_op jit(solution)/shard_map/ppermute | solution.py:303
  50.2 12.2 %collective-permute-start.6 = (bf16[4,16,16,128]{3,2,1,0:T(8,128)(2,1)S(1)}, bf16[4,16,16,128]{3,2,1,0:T(8,128)(2,1)S(1)}, u32[]{:S(2)}, u32[]{:S(2)}) collective-permute-start(bf16[4,16,16,128]{3,2,1,0:T(8,128)(2,1)S(1)} %collective-permute-done.5.refs_2_), channel_id=1, source_target_pairs={{0,1},{1,0},{2,3},{3,2},{4,5},{5,4},{6,7},{7,6},{8,9},{9,8},{10,11... | collective-permute-start | bytes 786440 | tf_op jit(solution)/shard_map/ppermute | solution.py:303
  50.3 14.0 %collective-permute-start.8 = (bf16[4,16,16,128]{3,2,1,0:T(8,128)(2,1)S(1)}, bf16[4,16,16,128]{3,2,1,0:T(8,128)(2,1)S(1)}, u32[]{:S(2)}, u32[]{:S(2)}) collective-permute-start(bf16[4,16,16,128]{3,2,1,0:T(8,128)(2,1)S(1)} %collective-permute-done.7.refs_4_), channel_id=1, source_target_pairs={{0,1},{1,0},{2,3},{3,2},{4,5},{5,4},{6,7},{7,6},{8,9},{9,8},{10,11... | collective-permute-start | bytes 786440 | tf_op jit(solution)/shard_map/ppermute | solution.py:303
  52.8 6.2 %collective-permute-start.21 = (f32[112,128]{1,0:T(8,128)}, f32[112,128]{1,0:T(8,128)S(1)}, u32[]{:S(2)}, u32[]{:S(2)}) collective-permute-start(f32[112,128]{1,0:T(8,128)} %get-tuple-element.38), channel_id=1, source_target_pairs={{0,24},{1,25},{2,26},{3,27},{4,28},{5,29},{6,30},{7,31},{8,16},{9,... | collective-permute-start | bytes 172040 | tf_op jit(solution)/shard_map/ppermute | solution.py:303
  59.0 28.7 %collective-permute-start.2 = (bf16[1,16,16,128]{3,2,1,0:T(8,128)(2,1)S(1)}, bf16[1,16,16,128]{3,2,1,0:T(8,128)(2,1)S(1)}, u32[]{:S(2)}, u32[]{:S(2)}) collective-permute-start(bf16[1,16,16,128]{3,2,1,0:T(8,128)(2,1)S(1)} %get-tuple-element.47), channel_id=1, source_target_pairs={{0,1},{1,2},{2,3},{3,4},{4,5},{5,6},{6,7},{7,8},{8,9},{9,10},{10,1... | collective-permute-start | bytes 196616 | tf_op jit(solution)/shard_map/ppermute | solution.py:306
  59.8 5.0 %collective-permute-start.22 = (f32[112,128]{1,0:T(8,128)S(1)}, f32[112,128]{1,0:T(8,128)S(1)}, u32[]{:S(2)}, u32[]{:S(2)}) collective-permute-start(f32[112,128]{1,0:T(8,128)S(1)} %add_add_fusion), channel_id=1, source_target_pairs={{0,8},{1,9},{2,10},{3,11},{4,12},{5,13},{6,14},{7,15},{8,0},{9,1},... | collective-permute-start | bytes 172040 | tf_op jit(solution)/shard_map/ppermute | solution.py:303
  59.9 7.4 %collective-permute-start.23 = (f32[112,128]{1,0:T(8,128)S(1)}, f32[112,128]{1,0:T(8,128)S(1)}, u32[]{:S(2)}, u32[]{:S(2)}) collective-permute-start(f32[112,128]{1,0:T(8,128)S(1)} %add_add_fusion), channel_id=1, source_target_pairs={{0,16},{1,17},{2,18},{3,19},{4,20},{5,21},{6,22},{7,23},{8,24},{9,... | collective-permute-start | bytes 172040 | tf_op jit(solution)/shard_map/ppermute | solution.py:303
  62.4 6.3 %collective-permute-start.24 = (f32[112,128]{1,0:T(8,128)S(1)}, f32[112,128]{1,0:T(8,128)S(1)}, u32[]{:S(2)}, u32[]{:S(2)}) collective-permute-start(f32[112,128]{1,0:T(8,128)S(1)} %add_add_fusion), channel_id=1, source_target_pairs={{0,24},{1,25},{2,26},{3,27},{4,28},{5,29},{6,30},{7,31},{8,16},{9,... | collective-permute-start | bytes 172040 | tf_op jit(solution)/shard_map/ppermute | solution.py:303
  64.4 8.3 %collective-permute-start.11 = (bf16[2,16,16,128]{3,2,1,0:T(8,128)(2,1)S(1)}, bf16[2,16,16,128]{3,2,1,0:T(8,128)(2,1)S(1)}, u32[]{:S(2)}, u32[]{:S(2)}) collective-permute-start(bf16[2,16,16,128]{3,2,1,0:T(8,128)(2,1)S(1)} %fusion.1), channel_id=1, source_target_pairs={{0,8},{1,9},{2,10},{3,11},{4,12},{5,13},{6,14},{7,15},{8,16},{9,17... | collective-permute-start | bytes 393224 | tf_op jit(solution)/shard_map/ppermute | solution.py:306
  68.7 23.3 %collective-permute-start.26 = (f32[448,128]{1,0:T(8,128)S(1)}, f32[448,128]{1,0:T(8,128)S(1)}, u32[]{:S(2)}, u32[]{:S(2)}) collective-permute-start(f32[448,128]{1,0:T(8,128)S(1)} %pad_maximum_fusion.refs_0_), channel_id=1, source_target_pairs={{0,2},{1,3},{2,0},{3,1},{4,6},{5,7},{6,4},{7,5},{8,10},{9,11},{10,... | collective-permute-start | bytes 688136 | tf_op jit(solution)/shard_map/ppermute | solution.py:303
  68.8 23.7 %collective-permute-start.28 = (f32[448,128]{1,0:T(8,128)S(1)}, f32[448,128]{1,0:T(8,128)S(1)}, u32[]{:S(2)}, u32[]{:S(2)}) collective-permute-start(f32[448,128]{1,0:T(8,128)S(1)} %pad_maximum_fusion.refs_0_), channel_id=1, source_target_pairs={{0,4},{1,5},{2,6},{3,7},{4,0},{5,1},{6,2},{7,3},{8,12},{9,13},{10,... | collective-permute-start | bytes 688136 | tf_op jit(solution)/shard_map/ppermute | solution.py:303
  71.2 21.3 %collective-permute-start.30 = (f32[448,128]{1,0:T(8,128)S(1)}, f32[448,128]{1,0:T(8,128)S(1)}, u32[]{:S(2)}, u32[]{:S(2)}) collective-permute-start(f32[448,128]{1,0:T(8,128)S(1)} %pad_maximum_fusion.refs_0_), channel_id=1, source_target_pairs={{0,6},{1,7},{2,4},{3,5},{4,2},{5,3},{6,0},{7,1},{8,14},{9,15},{10,... | collective-permute-start | bytes 688136 | tf_op jit(solution)/shard_map/ppermute | solution.py:303
  84.4 7.6 %collective-permute-start.12 = (f32[256,128]{1,0:T(8,128)S(1)}, f32[256,128]{1,0:T(8,128)S(1)}, u32[]{:S(2)}, u32[]{:S(2)}) collective-permute-start(f32[256,128]{1,0:T(8,128)S(1)} %get-tuple-element.26), channel_id=1, source_target_pairs={{0,8},{1,9},{2,10},{3,11},{4,12},{5,13},{6,14},{7,15},{8,0},{9,1},... | collective-permute-start | bytes 393224 | tf_op jit(solution)/shard_map/ppermute | solution.py:303
  87.7 3.2 %collective-permute-start.3 = (bf16[1,16,16,128]{3,2,1,0:T(8,128)(2,1)S(1)}, bf16[1,16,16,128]{3,2,1,0:T(8,128)(2,1)S(1)}, u32[]{:S(2)}, u32[]{:S(2)}) collective-permute-start(bf16[1,16,16,128]{3,2,1,0:T(8,128)(2,1)S(1)} %get-tuple-element.46), channel_id=1, source_target_pairs={{0,31},{1,0},{2,1},{3,2},{4,3},{5,4},{6,5},{7,6},{8,7},{9,8},{10,9... | collective-permute-start | bytes 196616 | tf_op jit(solution)/shard_map/ppermute | solution.py:306
  90.9 8.3 %collective-permute-start.13 = (f32[256,128]{1,0:T(8,128)S(1)}, f32[256,128]{1,0:T(8,128)S(1)}, u32[]{:S(2)}, u32[]{:S(2)}) collective-permute-start(f32[256,128]{1,0:T(8,128)S(1)} %get-tuple-element.27), channel_id=1, source_target_pairs={{0,16},{1,17},{2,18},{3,19},{4,20},{5,21},{6,22},{7,23},{8,24},{9,... | collective-permute-start | bytes 393224 | tf_op jit(solution)/shard_map/ppermute | solution.py:303
  92.0 19.6 %collective-permute-start.25 = (f32[448,128]{1,0:T(8,128)S(1)}, f32[448,128]{1,0:T(8,128)S(1)}, u32[]{:S(2)}, u32[]{:S(2)}) collective-permute-start(f32[448,128]{1,0:T(8,128)S(1)} %pad_maximum_fusion.refs_0_), channel_id=1, source_target_pairs={{0,1},{1,0},{2,3},{3,2},{4,5},{5,4},{6,7},{7,6},{8,9},{9,8},{10,11... | collective-permute-start | bytes 688136 | tf_op jit(solution)/shard_map/ppermute | solution.py:303
  92.0 19.6 %collective-permute-start.27 = (f32[448,128]{1,0:T(8,128)S(1)}, f32[448,128]{1,0:T(8,128)S(1)}, u32[]{:S(2)}, u32[]{:S(2)}) collective-permute-start(f32[448,128]{1,0:T(8,128)S(1)} %collective-permute-done.26.refs_2_), channel_id=1, source_target_pairs={{0,1},{1,0},{2,3},{3,2},{4,5},{5,4},{6,7},{7,6},{8,9},{9,8},{10,11... | collective-permute-start | bytes 688136 | tf_op jit(solution)/shard_map/ppermute | solution.py:303
  92.5 19.1 %collective-permute-start.29 = (f32[448,128]{1,0:T(8,128)S(1)}, f32[448,128]{1,0:T(8,128)S(1)}, u32[]{:S(2)}, u32[]{:S(2)}) collective-permute-start(f32[448,128]{1,0:T(8,128)S(1)} %collective-permute-done.28.refs_4_), channel_id=1, source_target_pairs={{0,1},{1,0},{2,3},{3,2},{4,5},{5,4},{6,7},{7,6},{8,9},{9,8},{10,11... | collective-permute-start | bytes 688136 | tf_op jit(solution)/shard_map/ppermute | solution.py:303
  92.6 19.0 %collective-permute-start.31 = (f32[448,128]{1,0:T(8,128)S(1)}, f32[448,128]{1,0:T(8,128)S(1)}, u32[]{:S(2)}, u32[]{:S(2)}) collective-permute-start(f32[448,128]{1,0:T(8,128)S(1)} %collective-permute-done.30.refs_6_), channel_id=1, source_target_pairs={{0,1},{1,0},{2,3},{3,2},{4,5},{5,4},{6,7},{7,6},{8,9},{9,8},{10,11... | collective-permute-start | bytes 688136 | tf_op jit(solution)/shard_map/ppermute | solution.py:303
  99.2 8.2 %collective-permute-start.14 = (f32[256,128]{1,0:T(8,128)S(1)}, f32[256,128]{1,0:T(8,128)S(1)}, u32[]{:S(2)}, u32[]{:S(2)}) collective-permute-start(f32[256,128]{1,0:T(8,128)S(1)} %get-tuple-element.28), channel_id=1, source_target_pairs={{0,24},{1,25},{2,26},{3,27},{4,28},{5,29},{6,30},{7,31},{8,16},{9,... | collective-permute-start | bytes 393224 | tf_op jit(solution)/shard_map/ppermute | solution.py:303
  (22 other events, 205.7 us)
